TPU v7x, 32 devices: a whole 2x2x4 slice. The times are simulated.
32 devices in a mesh: gx: 4 (over y, x), gy: 8 (over z, core).
Axes of the slice: x: 2, y: 2, z: 4, core: 2. Of those that a mesh axis runs over, the one named last changes fastest.
Arguments:
- start_block: bfloat16 [64, 65536], P(None, ('gx', 'gy')), may hold values from -200 to 200
- tiles: bfloat16 [256, 10, 256, 256], P(('gx', 'gy')), may hold values from -0.125 to 0.125
- tile_cols: int32 [256, 10], P(('gx', 'gy')), may hold values from 0 to 15, as said below
- send_rows: int32 [32, 2], P(('gx', 'gy')), may hold values from 0 to 7, as said below
- shifts: float32 [4], replicated, may hold values from -1 to 1
Outputs:
- basis_q: float32 [256, 65536], P(None, ('gx', 'gy'))
Inputs may be any that keep to these rules, and one draw needn't show every extreme that they name: `tile_cols`: every tile-row's first tile is its own diagonal tile; values below 8 name the partition's own tile-rows, the others ghost slots in the extended order. `send_rows`: each partition's 2 entries are distinct own tile-rows.
All inputs are finite; a program needn't handle non-finite values.
Results may differ from a plain program's by a relative error of at most 0.009.
The roundings to bfloat16 on the way count: a program that leaves them out, or rounds other values in their place, can miss the bound.
Values may be sent and summed in bfloat16 or wider, within the bound.
A program may use at most 64 MiB of HBM per device.

v0:
```python
import jax
import jax.numpy as jnp
from jax import lax
from jax.sharding import PartitionSpec as P


def extended_2(block, sides, width):
    for axis, dim in sides:
        count = lax.axis_size(axis)
        forward = [(i, i + 1) for i in range(count - 1)]
        backward = [(target, source) for source, target in forward]
        low = lax.ppermute(
            lax.slice_in_dim(block, block.shape[dim] - width, None, axis=dim), axis, forward
        )
        high = lax.ppermute(lax.slice_in_dim(block, 0, width, axis=dim), axis, backward)
        block = jnp.concatenate([low, block, high], axis=dim)
    return block


def apply_local(current, tiles, flat_cols, send_list):
    width = current.shape[0]
    tile_rows, slots, tile, _ = tiles.shape
    own = current.reshape(width, tile_rows, tile)
    outgoing = jnp.take(own, send_list, axis=1)
    framed = extended_2(outgoing[None, None], (("gx", 0), ("gy", 1)), 1)
    extended = jnp.concatenate(
        [own, framed[0, 1], framed[2, 1], framed[1, 0], framed[1, 2]], axis=1
    )
    picked = jnp.take(extended, flat_cols, axis=1).reshape(width, tile_rows, slots, tile)
    image = jnp.einsum("ctkb,tkab->cta", picked, tiles, preferred_element_type=jnp.float32)
    return image.reshape(width, tile_rows * tile)


def body(start_block, tiles, tile_cols, send_rows, shifts):
    flat_cols = tile_cols.reshape(-1)
    send_list = send_rows[0]
    current = start_block
    blocks = []
    for step in range(shifts.shape[0]):
        image = apply_local(current, tiles, flat_cols, send_list)
        current = (image - shifts[step] * current.astype(jnp.float32)).astype(jnp.bfloat16)
        blocks.append(current)
    basis = jnp.concatenate(blocks, axis=0)
    total_rows = basis.shape[1] * lax.axis_size("gx") * lax.axis_size("gy")
    local_gram = (
        lax.dot_general(basis, basis, (((1,), (1,)), ((), ())), preferred_element_type=jnp.float32)
        / total_rows
    )
    lower = jnp.linalg.cholesky(lax.psum(local_gram, ("gx", "gy")))
    return lax.linalg.triangular_solve(lower, basis.astype(jnp.float32), left_side=True, lower=True)


def solution(mesh):
    in_specs = (
        P(None, ("gx", "gy")),
        P(("gx", "gy"), None, None, None),
        P(("gx", "gy"), None),
        P(("gx", "gy"), None),
        P(),
    )
    out_specs = P(None, ("gx", "gy"))
    return jax.shard_map(body, mesh=mesh, in_specs=in_specs, out_specs=out_specs, check_vma=False)
```

profile of v0, /device:TPU:0, one launch (start us, length us, event | category | flops | bytes accessed | tf_op | source)
XLA Modules:
  0.0 325.0 jit_solution(11236422951529813700)
XLA Ops:
  9.5 1.3 collective-permute-start.1
  10.8 5.5 %collective-permute-start = (bf16[1,1,64,2,256]{4,2,3,1,0:T(8,128)(2,1)S(1)}, bf16[1,1,64,2,256]{4,2,3,1,0:T(8,128)(2,1)S(1)}, u32[]{:S(2)}, u32[]{:S(2)}) collective-permute-start(bf16[1,1,64,2,256]{4,2,3,1,0:T(8,128)(2,1)S(1)} %select_bitcast_fusion.3), channel_id=1, source_target_pairs={{0,8},{8,16},{16,24},{1,9},{9,17},{17,25},{2,10},{10,18},{18,26},{... | collective-permute-start | bytes 196616 | tf_op jit(solution)/shard_map/ppermute | solution.py:12
  18.0 1.5 fusion.28
  19.6 1.3 collective-permute-start.3
  20.9 3.0 collective-permute-start.2
  26.1 7.3 %convolution_bitcast_fusion.3 = f32[8,8,8,256]{3,2,1,0:T(8,128)S(1)} fusion(bf16[64,8,10,256]{3,0,2,1:T(8,128)(2,1)S(1)} %bitcast.176, bf16[8,10,256,256]{3,2,1,0:T(8,128)(2,1)} %param.10), kind=kOutput, calls=%fused_computation.19 | convolution fusion | flops 671088640 | bytes 13631488 | tf_op jit(solution)/shard_map/ctkb,tkab->cta/dot_general | solution.py:30
  34.7 1.3 collective-permute-start.5
  36.0 5.4 %collective-permute-start.4 = (bf16[1,1,64,2,256]{4,2,3,1,0:T(8,128)(2,1)S(1)}, bf16[1,1,64,2,256]{4,2,3,1,0:T(8,128)(2,1)S(1)}, u32[]{:S(2)}, u32[]{:S(2)}) collective-permute-start(bf16[1,1,64,2,256]{4,2,3,1,0:T(8,128)(2,1)S(1)} %select_bitcast_fusion.2), channel_id=1, source_target_pairs={{0,8},{8,16},{16,24},{1,9},{9,17},{17,25},{2,10},{10,18},{18,26},{... | collective-permute-start | bytes 196616 | tf_op jit(solution)/shard_map/ppermute | solution.py:12
  41.7 1.6 collective-permute-done.4
  43.4 1.3 collective-permute-start.7
  44.7 4.4 %collective-permute-start.6 = (bf16[3,1,64,2,256]{4,2,3,1,0:T(8,128)(2,1)S(1)}, bf16[3,1,64,2,256]{4,2,3,1,0:T(8,128)(2,1)S(1)}, u32[]{:S(2)}, u32[]{:S(2)}) collective-permute-start(bf16[3,1,64,2,256]{4,2,3,1,0:T(8,128)(2,1)S(1)} %pad_maximum_fusion.2), channel_id=1, source_target_pairs={{0,1},{1,2},{2,3},{3,4},{4,5},{5,6},{6,7},{8,9},{9,10},{10,11},{11... | collective-permute-start | bytes 589832 | tf_op jit(solution)/shard_map/ppermute | solution.py:12
  51.2 7.3 %convolution_bitcast_fusion.2 = f32[8,8,8,256]{3,2,1,0:T(8,128)S(1)} fusion(bf16[64,8,10,256]{3,0,2,1:T(8,128)(2,1)S(1)} %bitcast.177, bf16[8,10,256,256]{3,2,1,0:T(8,128)(2,1)} %param.10), kind=kOutput, calls=%fused_computation.18 | convolution fusion | flops 671088640 | bytes 13631488 | tf_op jit(solution)/shard_map/ctkb,tkab->cta/dot_general | solution.py:30
  59.9 1.3 collective-permute-start.9
  61.2 5.2 %collective-permute-start.8 = (bf16[1,1,64,2,256]{4,2,3,1,0:T(8,128)(2,1)S(1)}, bf16[1,1,64,2,256]{4,2,3,1,0:T(8,128)(2,1)S(1)}, u32[]{:S(2)}, u32[]{:S(2)}) collective-permute-start(bf16[1,1,64,2,256]{4,2,3,1,0:T(8,128)(2,1)S(1)} %select_bitcast_fusion.1), channel_id=1, source_target_pairs={{0,8},{8,16},{16,24},{1,9},{9,17},{17,25},{2,10},{10,18},{18,26},{... | collective-permute-start | bytes 196616 | tf_op jit(solution)/shard_map/ppermute | solution.py:12
  66.7 1.6 collective-permute-done.8
  68.3 1.3 collective-permute-start.11
  69.6 6.8 %collective-permute-start.10 = (bf16[3,1,64,2,256]{4,2,3,1,0:T(8,128)(2,1)S(1)}, bf16[3,1,64,2,256]{4,2,3,1,0:T(8,128)(2,1)S(1)}, u32[]{:S(2)}, u32[]{:S(2)}) collective-permute-start(bf16[3,1,64,2,256]{4,2,3,1,0:T(8,128)(2,1)S(1)} %pad_maximum_fusion.3), channel_id=1, source_target_pairs={{0,1},{1,2},{2,3},{3,4},{4,5},{5,6},{6,7},{8,9},{9,10},{10,11},{11... | collective-permute-start | bytes 589832 | tf_op jit(solution)/shard_map/ppermute | solution.py:12
  78.7 7.3 %convolution_bitcast_fusion.1 = f32[8,8,8,256]{3,2,1,0:T(8,128)S(1)} fusion(bf16[64,8,10,256]{3,0,2,1:T(8,128)(2,1)S(1)} %bitcast.178, bf16[8,10,256,256]{3,2,1,0:T(8,128)(2,1)} %param.10), kind=kOutput, calls=%fused_computation.17 | convolution fusion | flops 671088640 | bytes 13631488 | tf_op jit(solution)/shard_map/ctkb,tkab->cta/dot_general | solution.py:30
  88.7 5.8 %collective-permute-start.12 = (bf16[1,1,64,2,256]{4,2,3,1,0:T(8,128)(2,1)S(1)}, bf16[1,1,64,2,256]{4,2,3,1,0:T(8,128)(2,1)S(1)}, u32[]{:S(2)}, u32[]{:S(2)}) collective-permute-start(bf16[1,1,64,2,256]{4,2,3,1,0:T(8,128)(2,1)S(1)} %select_bitcast_fusion), channel_id=1, source_target_pairs={{0,8},{8,16},{16,24},{1,9},{9,17},{17,25},{2,10},{10,18},{18,26},{... | collective-permute-start | bytes 196616 | tf_op jit(solution)/shard_map/ppermute | solution.py:12
  94.8 1.6 collective-permute-done.12
  96.4 1.3 collective-permute-start.15
  97.7 6.8 %collective-permute-start.14 = (bf16[3,1,64,2,256]{4,2,3,1,0:T(8,128)(2,1)S(1)}, bf16[3,1,64,2,256]{4,2,3,1,0:T(8,128)(2,1)S(1)}, u32[]{:S(2)}, u32[]{:S(2)}) collective-permute-start(bf16[3,1,64,2,256]{4,2,3,1,0:T(8,128)(2,1)S(1)} %pad_maximum_fusion.4), channel_id=1, source_target_pairs={{0,1},{1,2},{2,3},{3,4},{4,5},{5,6},{6,7},{8,9},{9,10},{10,11},{11... | collective-permute-start | bytes 589832 | tf_op jit(solution)/shard_map/ppermute | solution.py:12
  106.5 7.3 %convolution_bitcast_fusion = f32[8,8,8,256]{3,2,1,0:T(8,128)S(1)} fusion(bf16[64,8,10,256]{3,0,2,1:T(8,128)(2,1)S(1)} %bitcast.175, bf16[8,10,256,256]{3,2,1,0:T(8,128)(2,1)} %param.10), kind=kOutput, calls=%fused_computation.16 | convolution fusion | flops 671088640 | bytes 13631488 | tf_op jit(solution)/shard_map/ctkb,tkab->cta/dot_general | solution.py:30
  115.8 136.7 %all-reduce.3.cloned.1.call-done = f32[256,256]{0,1:T(8,128)} async-done(((f32[256,256]{0,1:T(8,128)}), f32[256,256]{0,1:T(8,128)}) %all-reduce.3.cloned.1.call-update) | async-done | bytes 262160 | tf_op jit(solution)/shard_map/psum | solution.py:49
  254.6 11.7 %cholesky.50 = f32[128,128]{1,0:T(8,128)S(1)} custom-call(f32[128,128]{1,0:T(8,128)S(1)} %cholesky.118), custom_call_target="Cholesky" | custom-call | tf_op jit(solution)/shard_map/jit(cholesky)/cholesky | solution.py:49
  266.4 9.8 %custom-call.14 = f32[1,128,128]{1,2,0:T(8,128)S(1)} custom-call(f32[1,128,128]{2,1,0:T(8,128)S(1)} %get-tuple-element.28), custom_call_target="InvertDiagBlocksLowerTriangular" | custom-call | tf_op jit(solution)/shard_map/jit(cholesky)/cholesky | solution.py:49
  276.7 11.9 %cholesky.105 = f32[128,128]{1,0:T(8,128)S(1)} custom-call(f32[128,128]{1,0:T(8,128)S(1)} %convolution_subtract_fusion.1), custom_call_target="Cholesky" | custom-call | tf_op jit(solution)/shard_map/jit(cholesky)/cholesky | solution.py:49
  290.5 3.8 %while.1 = (s32[]{:T(128)}, f32[256,256]{1,0:T(8,128)S(1)}, s32[2,2]{1,0:T(2,128)S(1)}, f32[2,128,128]{2,1,0:T(8,128)S(1)}, s32[]{:T(128)}) while((s32[]{:T(128)}, f32[256,256]{1,0:T(8,128)S(1)}, s32[2,2]{1,0:T(2,128)S(1)}, f32[2,128,128]{2,1,0:T(8,128)S(1)}, s32[]{:T(128)}) %tuple.28), condition=%wide.while_cond, body=%wide.while_body.sunk | while | flops 2 | bytes 131189 | solution.py:50
  291.1 1.3 bitcast_dynamic-update-slice_fusion.10
  293.0 1.3 bitcast_dynamic-update-slice_fusion.10
  294.3 19.7 %custom-call.15 = f32[2,128,128]{1,2,0:T(8,128)S(1)} custom-call(f32[2,128,128]{2,1,0:T(8,128)S(1)} %get-tuple-element.14), custom_call_target="InvertDiagBlocksLowerTriangular" | custom-call | tf_op jit(solution)/shard_map/triangular_solve | solution.py:50
  316.7 1.5 pad_maximum_fusion
  (108 shorter events, 28.6 us)
Async XLA Ops:
  6.5 246.0 %all-reduce.3.cloned.1.call-start = ((), (), s32[]{:S(2)}) async-start(), calls=%async_computation | async-start | bytes 524288 | tf_op jit(solution)/shard_map/psum | solution.py:49
  9.5 10.0 %collective-permute-start.1 = (bf16[1,1,64,2,256]{4,2,3,1,0:T(8,128)(2,1)S(1)}, bf16[1,1,64,2,256]{4,2,3,1,0:T(8,128)(2,1)S(1)}, u32[]{:S(2)}, u32[]{:S(2)}) collective-permute-start(bf16[1,1,64,2,256]{4,2,3,1,0:T(8,128)(2,1)S(1)} %select_bitcast_fusion.3), channel_id=1, source_target_pairs={{8,0},{16,8},{24,16},{9,1},{17,9},{25,17},{10,2},{18,10},{26,18},{... | collective-permute-start | bytes 196616 | tf_op jit(solution)/shard_map/ppermute | solution.py:15
  10.8 8.8 %collective-permute-start = (bf16[1,1,64,2,256]{4,2,3,1,0:T(8,128)(2,1)S(1)}, bf16[1,1,64,2,256]{4,2,3,1,0:T(8,128)(2,1)S(1)}, u32[]{:S(2)}, u32[]{:S(2)}) collective-permute-start(bf16[1,1,64,2,256]{4,2,3,1,0:T(8,128)(2,1)S(1)} %select_bitcast_fusion.3), channel_id=1, source_target_pairs={{0,8},{8,16},{16,24},{1,9},{9,17},{17,25},{2,10},{10,18},{18,26},{... | collective-permute-start | bytes 196616 | tf_op jit(solution)/shard_map/ppermute | solution.py:12
  19.6 5.4 %collective-permute-start.3 = (bf16[3,1,64,2,256]{4,2,3,1,0:T(8,128)(2,1)S(1)}, bf16[3,1,64,2,256]{4,2,3,1,0:T(8,128)(2,1)S(1)}, u32[]{:S(2)}, u32[]{:S(2)}) collective-permute-start(bf16[3,1,64,2,256]{4,2,3,1,0:T(8,128)(2,1)S(1)} %pad_maximum_fusion.1), channel_id=1, source_target_pairs={{1,0},{2,1},{3,2},{4,3},{5,4},{6,5},{7,6},{9,8},{10,9},{11,10},{12... | collective-permute-start | bytes 589832 | tf_op jit(solution)/shard_map/ppermute | solution.py:15
  20.9 4.1 %collective-permute-start.2 = (bf16[3,1,64,2,256]{4,2,3,1,0:T(8,128)(2,1)S(1)}, bf16[3,1,64,2,256]{4,2,3,1,0:T(8,128)(2,1)S(1)}, u32[]{:S(2)}, u32[]{:S(2)}) collective-permute-start(bf16[3,1,64,2,256]{4,2,3,1,0:T(8,128)(2,1)S(1)} %pad_maximum_fusion.1), channel_id=1, source_target_pairs={{0,1},{1,2},{2,3},{3,4},{4,5},{5,6},{6,7},{8,9},{9,10},{10,11},{11... | collective-permute-start | bytes 589832 | tf_op jit(solution)/shard_map/ppermute | solution.py:12
  26.1 7.3 %copy-start.5 = (bf16[64,2048]{1,0:T(8,128)(2,1)S(1)}, bf16[64,2048]{1,0:T(8,128)(2,1)}, u32[]{:S(2)}) copy-start(bf16[64,2048]{1,0:T(8,128)(2,1)} %param.9) | copy-start | bytes 786436
  34.7 7.0 %collective-permute-start.5 = (bf16[1,1,64,2,256]{4,2,3,1,0:T(8,128)(2,1)S(1)}, bf16[1,1,64,2,256]{4,2,3,1,0:T(8,128)(2,1)S(1)}, u32[]{:S(2)}, u32[]{:S(2)}) collective-permute-start(bf16[1,1,64,2,256]{4,2,3,1,0:T(8,128)(2,1)S(1)} %select_bitcast_fusion.2), channel_id=1, source_target_pairs={{8,0},{16,8},{24,16},{9,1},{17,9},{25,17},{10,2},{18,10},{26,18},{... | collective-permute-start | bytes 196616 | tf_op jit(solution)/shard_map/ppermute | solution.py:15
  36.0 7.3 %collective-permute-start.4 = (bf16[1,1,64,2,256]{4,2,3,1,0:T(8,128)(2,1)S(1)}, bf16[1,1,64,2,256]{4,2,3,1,0:T(8,128)(2,1)S(1)}, u32[]{:S(2)}, u32[]{:S(2)}) collective-permute-start(bf16[1,1,64,2,256]{4,2,3,1,0:T(8,128)(2,1)S(1)} %select_bitcast_fusion.2), channel_id=1, source_target_pairs={{0,8},{8,16},{16,24},{1,9},{9,17},{17,25},{2,10},{10,18},{18,26},{... | collective-permute-start | bytes 196616 | tf_op jit(solution)/shard_map/ppermute | solution.py:12
  43.4 6.8 %collective-permute-start.7 = (bf16[3,1,64,2,256]{4,2,3,1,0:T(8,128)(2,1)S(1)}, bf16[3,1,64,2,256]{4,2,3,1,0:T(8,128)(2,1)S(1)}, u32[]{:S(2)}, u32[]{:S(2)}) collective-permute-start(bf16[3,1,64,2,256]{4,2,3,1,0:T(8,128)(2,1)S(1)} %pad_maximum_fusion.2), channel_id=1, source_target_pairs={{1,0},{2,1},{3,2},{4,3},{5,4},{6,5},{7,6},{9,8},{10,9},{11,10},{12... | collective-permute-start | bytes 589832 | tf_op jit(solution)/shard_map/ppermute | solution.py:15
  44.7 5.5 %collective-permute-start.6 = (bf16[3,1,64,2,256]{4,2,3,1,0:T(8,128)(2,1)S(1)}, bf16[3,1,64,2,256]{4,2,3,1,0:T(8,128)(2,1)S(1)}, u32[]{:S(2)}, u32[]{:S(2)}) collective-permute-start(bf16[3,1,64,2,256]{4,2,3,1,0:T(8,128)(2,1)S(1)} %pad_maximum_fusion.2), channel_id=1, source_target_pairs={{0,1},{1,2},{2,3},{3,4},{4,5},{5,6},{6,7},{8,9},{9,10},{10,11},{11... | collective-permute-start | bytes 589832 | tf_op jit(solution)/shard_map/ppermute | solution.py:12
  59.3 18.3 %copy-start = (bf16[64,2048]{1,0:T(8,128)(2,1)}, bf16[64,2048]{1,0:T(8,128)(2,1)S(1)}, u32[]{:S(2)}) copy-start(bf16[64,2048]{1,0:T(8,128)(2,1)S(1)} %subtract_convert_fusion.2) | copy-start | bytes 786436
  59.9 6.8 %collective-permute-start.9 = (bf16[1,1,64,2,256]{4,2,3,1,0:T(8,128)(2,1)S(1)}, bf16[1,1,64,2,256]{4,2,3,1,0:T(8,128)(2,1)S(1)}, u32[]{:S(2)}, u32[]{:S(2)}) collective-permute-start(bf16[1,1,64,2,256]{4,2,3,1,0:T(8,128)(2,1)S(1)} %select_bitcast_fusion.1), channel_id=1, source_target_pairs={{8,0},{16,8},{24,16},{9,1},{17,9},{25,17},{10,2},{18,10},{26,18},{... | collective-permute-start | bytes 196616 | tf_op jit(solution)/shard_map/ppermute | solution.py:15
  61.2 7.1 %collective-permute-start.8 = (bf16[1,1,64,2,256]{4,2,3,1,0:T(8,128)(2,1)S(1)}, bf16[1,1,64,2,256]{4,2,3,1,0:T(8,128)(2,1)S(1)}, u32[]{:S(2)}, u32[]{:S(2)}) collective-permute-start(bf16[1,1,64,2,256]{4,2,3,1,0:T(8,128)(2,1)S(1)} %select_bitcast_fusion.1), channel_id=1, source_target_pairs={{0,8},{8,16},{16,24},{1,9},{9,17},{17,25},{2,10},{10,18},{18,26},{... | collective-permute-start | bytes 196616 | tf_op jit(solution)/shard_map/ppermute | solution.py:12
  68.3 9.2 %collective-permute-start.11 = (bf16[3,1,64,2,256]{4,2,3,1,0:T(8,128)(2,1)S(1)}, bf16[3,1,64,2,256]{4,2,3,1,0:T(8,128)(2,1)S(1)}, u32[]{:S(2)}, u32[]{:S(2)}) collective-permute-start(bf16[3,1,64,2,256]{4,2,3,1,0:T(8,128)(2,1)S(1)} %pad_maximum_fusion.3), channel_id=1, source_target_pairs={{1,0},{2,1},{3,2},{4,3},{5,4},{6,5},{7,6},{9,8},{10,9},{11,10},{12... | collective-permute-start | bytes 589832 | tf_op jit(solution)/shard_map/ppermute | solution.py:15
  69.6 7.9 %collective-permute-start.10 = (bf16[3,1,64,2,256]{4,2,3,1,0:T(8,128)(2,1)S(1)}, bf16[3,1,64,2,256]{4,2,3,1,0:T(8,128)(2,1)S(1)}, u32[]{:S(2)}, u32[]{:S(2)}) collective-permute-start(bf16[3,1,64,2,256]{4,2,3,1,0:T(8,128)(2,1)S(1)} %pad_maximum_fusion.3), channel_id=1, source_target_pairs={{0,1},{1,2},{2,3},{3,4},{4,5},{5,6},{6,7},{8,9},{9,10},{10,11},{11... | collective-permute-start | bytes 589832 | tf_op jit(solution)/shard_map/ppermute | solution.py:12
  78.6 7.3 %copy-start.1 = (bf16[64,2048]{1,0:T(8,128)(2,1)S(1)}, bf16[64,2048]{1,0:T(8,128)(2,1)}, u32[]{:S(2)}) copy-start(bf16[64,2048]{1,0:T(8,128)(2,1)} %copy-done) | copy-start | bytes 786436
  86.8 18.6 %copy-start.3 = (bf16[64,2048]{1,0:T(8,128)(2,1)}, bf16[64,2048]{1,0:T(8,128)(2,1)S(1)}, u32[]{:S(2)}) copy-start(bf16[64,2048]{1,0:T(8,128)(2,1)S(1)} %subtract_convert_fusion.1) | copy-start | bytes 786436
  87.4 7.4 %collective-permute-start.13 = (bf16[1,1,64,2,256]{4,2,3,1,0:T(8,128)(2,1)S(1)}, bf16[1,1,64,2,256]{4,2,3,1,0:T(8,128)(2,1)S(1)}, u32[]{:S(2)}, u32[]{:S(2)}) collective-permute-start(bf16[1,1,64,2,256]{4,2,3,1,0:T(8,128)(2,1)S(1)} %select_bitcast_fusion), channel_id=1, source_target_pairs={{8,0},{16,8},{24,16},{9,1},{17,9},{25,17},{10,2},{18,10},{26,18},{... | collective-permute-start | bytes 196616 | tf_op jit(solution)/shard_map/ppermute | solution.py:15
  88.7 7.7 %collective-permute-start.12 = (bf16[1,1,64,2,256]{4,2,3,1,0:T(8,128)(2,1)S(1)}, bf16[1,1,64,2,256]{4,2,3,1,0:T(8,128)(2,1)S(1)}, u32[]{:S(2)}, u32[]{:S(2)}) collective-permute-start(bf16[1,1,64,2,256]{4,2,3,1,0:T(8,128)(2,1)S(1)} %select_bitcast_fusion), channel_id=1, source_target_pairs={{0,8},{8,16},{16,24},{1,9},{9,17},{17,25},{2,10},{10,18},{18,26},{... | collective-permute-start | bytes 196616 | tf_op jit(solution)/shard_map/ppermute | solution.py:12
  96.4 8.9 %collective-permute-start.15 = (bf16[3,1,64,2,256]{4,2,3,1,0:T(8,128)(2,1)S(1)}, bf16[3,1,64,2,256]{4,2,3,1,0:T(8,128)(2,1)S(1)}, u32[]{:S(2)}, u32[]{:S(2)}) collective-permute-start(bf16[3,1,64,2,256]{4,2,3,1,0:T(8,128)(2,1)S(1)} %pad_maximum_fusion.4), channel_id=1, source_target_pairs={{1,0},{2,1},{3,2},{4,3},{5,4},{6,5},{7,6},{9,8},{10,9},{11,10},{12... | collective-permute-start | bytes 589832 | tf_op jit(solution)/shard_map/ppermute | solution.py:15
  97.7 7.6 %collective-permute-start.14 = (bf16[3,1,64,2,256]{4,2,3,1,0:T(8,128)(2,1)S(1)}, bf16[3,1,64,2,256]{4,2,3,1,0:T(8,128)(2,1)S(1)}, u32[]{:S(2)}, u32[]{:S(2)}) collective-permute-start(bf16[3,1,64,2,256]{4,2,3,1,0:T(8,128)(2,1)S(1)} %pad_maximum_fusion.4), channel_id=1, source_target_pairs={{0,1},{1,2},{2,3},{3,4},{4,5},{5,6},{6,7},{8,9},{9,10},{10,11},{11... | collective-permute-start | bytes 589832 | tf_op jit(solution)/shard_map/ppermute | solution.py:12
  106.5 7.4 %copy-start.4 = (bf16[64,2048]{1,0:T(8,128)(2,1)S(1)}, bf16[64,2048]{1,0:T(8,128)(2,1)}, u32[]{:S(2)}) copy-start(bf16[64,2048]{1,0:T(8,128)(2,1)} %copy-done.3) | copy-start | bytes 786436
  106.5 8.1 %copy-start.2 = (bf16[64,2048]{1,0:T(8,128)(2,1)S(1)}, bf16[64,2048]{1,0:T(8,128)(2,1)}, u32[]{:S(2)}) copy-start(bf16[64,2048]{1,0:T(8,128)(2,1)} %copy-done) | copy-start | bytes 786436
Sparse Core Ops, SparseCore 0:
  115.9 136.5 all-reduce.2
where the time goes:
time: 326 us; the launch traced here: 325 us
  waiting for transfers between devices  146 us (45%)
  other arithmetic  62.1 us (19%)
  starting transfers between devices  53.3 us (16%)
  matrix products  33.4 us (10%)
  between operations  15.3 us (5%)
  local copies, waits for them, and re-layouts  14.7 us (5%)
    psum x1, waiting for transfers between devices, body(): lower = jnp.linalg.cholesky(lax.psum(local_gram, ('gx', 'gy')))  137 us
    ppermute x8, starting transfers between devices, extended_2(): lax.ppermute(lax.slice_in_dim(block, block.shape[dim] - width, None, axis...  43 us
    another operation x6, other arithmetic, body(): lower = jnp.linalg.cholesky(lax.psum(local_gram, ('gx', 'gy')))  34.1 us
    dot_general x4, matrix products, apply_local(): jnp.einsum('ctkb,tkab->cta', picked, tiles, preferred_element_type=jnp.fl...  29.1 us
    another operation x4, other arithmetic, body(): lax.linalg.triangular_solve(lower, basis.astype(jnp.float32), left_side=T...  21.2 us
    ppermute x8, starting transfers between devices, extended_2(): lax.ppermute(lax.slice_in_dim(block, 0, width, axis=dim), axis, backward)  10.3 us
    ppermute x8, waiting for transfers between devices, extended_2(): lax.ppermute(lax.slice_in_dim(block, block.shape[dim] - width, None, axis...  8.61 us
  transfers between devices with their start and end apart: 17, of which 11 were waited for; matrix products, arithmetic and copies ran while one was open for 1% of the time, Pallas kernels for 0%

commit v1 on v0

--- a/solution.py
+++ b/solution.py
@@ -46,7 +46,7 @@
         lax.dot_general(basis, basis, (((1,), (1,)), ((), ())), preferred_element_type=jnp.float32)
         / total_rows
     )
-    lower = jnp.linalg.cholesky(lax.psum(local_gram, ("gx", "gy")))
+    lower = jnp.linalg.cholesky(jnp.sum(lax.all_gather(local_gram, ("gx", "gy")), axis=0))
     return lax.linalg.triangular_solve(lower, basis.astype(jnp.float32), left_side=True, lower=True)
 
 

time: 326 us -> 278 us (0.85)
  waiting for transfers between devices: 146 us -> 109 us
  starting transfers between devices: 53.3 us -> 40.6 us
    psum x1 -> x0, waiting for transfers between devices: 137 us -> none  [body(): lower = jnp.linalg.cholesky(lax.psum(local_gram, ('gx', 'gy')))]
    all_gather x0 -> x1, waiting for transfers between devices: none -> 79.5 us  [body(): lax.all_gather(local_gram, ('gx', 'gy'))]
    ppermute x8, waiting for transfers between devices: 0.84 us -> 27.4 us  [extended_2(): lax.ppermute(lax.slice_in_dim(block, 0, width, axis=dim), axis, backward)]
    ppermute x8, starting transfers between devices: 43 us -> 30.1 us  [extended_2(): lax.ppermute(lax.slice_in_dim(block, block.shape[dim] - width, None, axis...]
    ppermute x8, waiting for transfers between devices: 8.61 us -> 1.69 us  [extended_2(): lax.ppermute(lax.slice_in_dim(block, block.shape[dim] - width, None, axis...]
    reduce_sum x0 -> x1, other arithmetic: none -> 3.93 us  [body(): jnp.sum(lax.all_gather(local_gram, ('gx', 'gy')), axis=0)]
  transfers between devices with their start and end apart: 17 -> 17, of which waited for: 11 -> 12; matrix products, arithmetic and copies ran while one was open for 1% -> 1% of each run, Pallas kernels for 0% -> 0%
where the time goes in v1:
time: 278 us; the launch traced here: 277 us
  waiting for transfers between devices  109 us (39%)
  other arithmetic  65.1 us (23%)
  starting transfers between devices  40.6 us (15%)
  matrix products  33.4 us (12%)
  between operations  15.3 us (6%)
  local copies, waits for them, and re-layouts  13.8 us (5%)
    all_gather x1, waiting for transfers between devices, body(): lax.all_gather(local_gram, ('gx', 'gy'))  79.5 us
    another operation x6, other arithmetic, body(): jnp.linalg.cholesky(jnp.sum(lax.all_gather(local_gram, ('gx', 'gy')), axi...  34.2 us
    ppermute x8, starting transfers between devices, extended_2(): lax.ppermute(lax.slice_in_dim(block, block.shape[dim] - width, None, axis...  30.1 us
    dot_general x4, matrix products, apply_local(): jnp.einsum('ctkb,tkab->cta', picked, tiles, preferred_element_type=jnp.fl...  29.1 us
    ppermute x8, waiting for transfers between devices, extended_2(): lax.ppermute(lax.slice_in_dim(block, 0, width, axis=dim), axis, backward)  27.4 us
    another operation x4, other arithmetic, body(): lax.linalg.triangular_solve(lower, basis.astype(jnp.float32), left_side=T...  21.2 us
    ppermute x8, starting transfers between devices, extended_2(): lax.ppermute(lax.slice_in_dim(block, 0, width, axis=dim), axis, backward)  10.5 us
  transfers between devices with their start and end apart: 17, of which 12 were waited for; matrix products, arithmetic and copies ran while one was open for 1% of the time, Pallas kernels for 0%

profile of v1, /device:TPU:0, one launch (start us, length us, event | category | flops | bytes accessed | tf_op | source)
XLA Modules:
  0.0 276.8 jit_solution(18047211156065949003)
XLA Ops:
  9.5 4.9 %collective-permute-start = (bf16[1,1,64,2,256]{4,2,3,1,0:T(8,128)(2,1)S(1)}, bf16[1,1,64,2,256]{4,2,3,1,0:T(8,128)(2,1)S(1)}, u32[]{:S(2)}, u32[]{:S(2)}) collective-permute-start(bf16[1,1,64,2,256]{4,2,3,1,0:T(8,128)(2,1)S(1)} %select_bitcast_fusion.3), channel_id=1, source_target_pairs={{0,8},{8,16},{16,24},{1,9},{9,17},{17,25},{2,10},{10,18},{18,26},{... | collective-permute-start | bytes 196616 | tf_op jit(solution)/shard_map/ppermute | solution.py:12
  14.3 1.3 collective-permute-start.1
  17.4 1.5 fusion.28
  18.9 1.6 collective-permute-done.1
  20.5 1.3 collective-permute-start.2
  21.8 1.3 collective-permute-start.3
  23.2 3.8 %collective-permute-done.3 = bf16[3,1,64,2,256]{4,2,3,1,0:T(8,128)(2,1)S(1)} collective-permute-done((bf16[3,1,64,2,256]{4,2,3,1,0:T(8,128)(2,1)S(1)}, bf16[3,1,64,2,256]{4,2,3,1,0:T(8,128)(2,1)S(1)}, u32[]{:S(2)}, u32[]{:S(2)}) %collective-permute-start.3) | collective-permute-done | bytes 196640 | tf_op jit(solution)/shard_map/ppermute | solution.py:15
  28.1 7.3 %convolution_bitcast_fusion.3 = f32[8,8,8,256]{3,2,1,0:T(8,128)S(1)} fusion(bf16[64,8,10,256]{3,0,2,1:T(8,128)(2,1)S(1)} %bitcast.177, bf16[8,10,256,256]{3,2,1,0:T(8,128)(2,1)} %param.10), kind=kOutput, calls=%fused_computation.19 | convolution fusion | flops 671088640 | bytes 13631488 | tf_op jit(solution)/shard_map/ctkb,tkab->cta/dot_general | solution.py:30
  36.7 4.3 %collective-permute-start.4 = (bf16[1,1,64,2,256]{4,2,3,1,0:T(8,128)(2,1)S(1)}, bf16[1,1,64,2,256]{4,2,3,1,0:T(8,128)(2,1)S(1)}, u32[]{:S(2)}, u32[]{:S(2)}) collective-permute-start(bf16[1,1,64,2,256]{4,2,3,1,0:T(8,128)(2,1)S(1)} %select_bitcast_fusion.2), channel_id=1, source_target_pairs={{0,8},{8,16},{16,24},{1,9},{9,17},{17,25},{2,10},{10,18},{18,26},{... | collective-permute-start | bytes 196616 | tf_op jit(solution)/shard_map/ppermute | solution.py:12
  42.9 4.7 %collective-permute-done.5 = bf16[1,1,64,2,256]{4,2,3,1,0:T(8,128)(2,1)S(1)} collective-permute-done((bf16[1,1,64,2,256]{4,2,3,1,0:T(8,128)(2,1)S(1)}, bf16[1,1,64,2,256]{4,2,3,1,0:T(8,128)(2,1)S(1)}, u32[]{:S(2)}, u32[]{:S(2)}) %collective-permute-start.5) | collective-permute-done | bytes 65568 | tf_op jit(solution)/shard_map/ppermute | solution.py:15
  47.6 4.2 %collective-permute-start.6 = (bf16[3,1,64,2,256]{4,2,3,1,0:T(8,128)(2,1)S(1)}, bf16[3,1,64,2,256]{4,2,3,1,0:T(8,128)(2,1)S(1)}, u32[]{:S(2)}, u32[]{:S(2)}) collective-permute-start(bf16[3,1,64,2,256]{4,2,3,1,0:T(8,128)(2,1)S(1)} %pad_maximum_fusion.2), channel_id=1, source_target_pairs={{0,1},{1,2},{2,3},{3,4},{4,5},{5,6},{6,7},{8,9},{9,10},{10,11},{11... | collective-permute-start | bytes 589832 | tf_op jit(solution)/shard_map/ppermute | solution.py:12
  53.2 2.8 %collective-permute-done.7 = bf16[3,1,64,2,256]{4,2,3,1,0:T(8,128)(2,1)S(1)} collective-permute-done((bf16[3,1,64,2,256]{4,2,3,1,0:T(8,128)(2,1)S(1)}, bf16[3,1,64,2,256]{4,2,3,1,0:T(8,128)(2,1)S(1)}, u32[]{:S(2)}, u32[]{:S(2)}) %collective-permute-start.7) | collective-permute-done | bytes 196640 | tf_op jit(solution)/shard_map/ppermute | solution.py:15
  57.1 7.2 %convolution_bitcast_fusion.2 = f32[8,8,8,256]{3,2,1,0:T(8,128)S(1)} fusion(bf16[64,8,10,256]{3,0,2,1:T(8,128)(2,1)S(1)} %bitcast.178, bf16[8,10,256,256]{3,2,1,0:T(8,128)(2,1)} %param.10), kind=kOutput, calls=%fused_computation.18 | convolution fusion | flops 671088640 | bytes 13631488 | tf_op jit(solution)/shard_map/ctkb,tkab->cta/dot_general | solution.py:30
  65.8 3.9 %collective-permute-start.8 = (bf16[1,1,64,2,256]{4,2,3,1,0:T(8,128)(2,1)S(1)}, bf16[1,1,64,2,256]{4,2,3,1,0:T(8,128)(2,1)S(1)}, u32[]{:S(2)}, u32[]{:S(2)}) collective-permute-start(bf16[1,1,64,2,256]{4,2,3,1,0:T(8,128)(2,1)S(1)} %select_bitcast_fusion.1), channel_id=1, source_target_pairs={{0,8},{8,16},{16,24},{1,9},{9,17},{17,25},{2,10},{10,18},{18,26},{... | collective-permute-start | bytes 196616 | tf_op jit(solution)/shard_map/ppermute | solution.py:12
  71.5 4.5 %collective-permute-done.9 = bf16[1,1,64,2,256]{4,2,3,1,0:T(8,128)(2,1)S(1)} collective-permute-done((bf16[1,1,64,2,256]{4,2,3,1,0:T(8,128)(2,1)S(1)}, bf16[1,1,64,2,256]{4,2,3,1,0:T(8,128)(2,1)S(1)}, u32[]{:S(2)}, u32[]{:S(2)}) %collective-permute-start.9) | collective-permute-done | bytes 65568 | tf_op jit(solution)/shard_map/ppermute | solution.py:15
  76.1 4.4 %collective-permute-start.10 = (bf16[3,1,64,2,256]{4,2,3,1,0:T(8,128)(2,1)S(1)}, bf16[3,1,64,2,256]{4,2,3,1,0:T(8,128)(2,1)S(1)}, u32[]{:S(2)}, u32[]{:S(2)}) collective-permute-start(bf16[3,1,64,2,256]{4,2,3,1,0:T(8,128)(2,1)S(1)} %pad_maximum_fusion.3), channel_id=1, source_target_pairs={{0,1},{1,2},{2,3},{3,4},{4,5},{5,6},{6,7},{8,9},{9,10},{10,11},{11... | collective-permute-start | bytes 589832 | tf_op jit(solution)/shard_map/ppermute | solution.py:12
  81.8 2.8 %collective-permute-done.11 = bf16[3,1,64,2,256]{4,2,3,1,0:T(8,128)(2,1)S(1)} collective-permute-done((bf16[3,1,64,2,256]{4,2,3,1,0:T(8,128)(2,1)S(1)}, bf16[3,1,64,2,256]{4,2,3,1,0:T(8,128)(2,1)S(1)}, u32[]{:S(2)}, u32[]{:S(2)}) %collective-permute-start.11) | collective-permute-done | bytes 196640 | tf_op jit(solution)/shard_map/ppermute | solution.py:15
  85.8 7.3 %convolution_bitcast_fusion.1 = f32[8,8,8,256]{3,2,1,0:T(8,128)S(1)} fusion(bf16[64,8,10,256]{3,0,2,1:T(8,128)(2,1)S(1)} %bitcast.179, bf16[8,10,256,256]{3,2,1,0:T(8,128)(2,1)} %param.10), kind=kOutput, calls=%fused_computation.17 | convolution fusion | flops 671088640 | bytes 13631488 | tf_op jit(solution)/shard_map/ctkb,tkab->cta/dot_general | solution.py:30
  94.6 2.7 collective-permute-start.12
  99.2 4.5 %collective-permute-done.13 = bf16[1,1,64,2,256]{4,2,3,1,0:T(8,128)(2,1)S(1)} collective-permute-done((bf16[1,1,64,2,256]{4,2,3,1,0:T(8,128)(2,1)S(1)}, bf16[1,1,64,2,256]{4,2,3,1,0:T(8,128)(2,1)S(1)}, u32[]{:S(2)}, u32[]{:S(2)}) %collective-permute-start.13) | collective-permute-done | bytes 65568 | tf_op jit(solution)/shard_map/ppermute | solution.py:15
  103.7 4.4 %collective-permute-start.14 = (bf16[3,1,64,2,256]{4,2,3,1,0:T(8,128)(2,1)S(1)}, bf16[3,1,64,2,256]{4,2,3,1,0:T(8,128)(2,1)S(1)}, u32[]{:S(2)}, u32[]{:S(2)}) collective-permute-start(bf16[3,1,64,2,256]{4,2,3,1,0:T(8,128)(2,1)S(1)} %pad_maximum_fusion.4), channel_id=1, source_target_pairs={{0,1},{1,2},{2,3},{3,4},{4,5},{5,6},{6,7},{8,9},{9,10},{10,11},{11... | collective-permute-start | bytes 589832 | tf_op jit(solution)/shard_map/ppermute | solution.py:12
  108.1 1.5 collective-permute-start.15
  109.6 2.7 collective-permute-done.15
  113.4 7.3 %convolution_bitcast_fusion = f32[8,8,8,256]{3,2,1,0:T(8,128)S(1)} fusion(bf16[64,8,10,256]{3,0,2,1:T(8,128)(2,1)S(1)} %bitcast.176, bf16[8,10,256,256]{3,2,1,0:T(8,128)(2,1)} %param.10), kind=kOutput, calls=%fused_computation.16 | convolution fusion | flops 671088640 | bytes 13631488 | tf_op jit(solution)/shard_map/ctkb,tkab->cta/dot_general | solution.py:30
  122.7 79.5 %all-gather.3.cloned.1.call-done = f32[8192,256]{1,0:T(8,128)} async-done(((f32[256,256]{1,0:T(8,128)}), f32[8192,256]{1,0:T(8,128)}) %all-gather.3.cloned.1.call-update) | async-done | bytes 8388624 | tf_op jit(solution)/shard_map/all_gather | solution.py:49
  202.2 3.9 %reduce_sum.9 = f32[256,256]{1,0:T(8,128)S(1)} reduce(f32[32,256,256]{2,1,0:T(8,128)} %bitcast.180, f32[]{:T(128)} %constant.95.clone.1), dimensions={0}, to_apply=%region_0.3 | reduce | flops 2031616 | bytes 8650756 | tf_op jit(solution)/shard_map/reduce_sum | solution.py:49
  206.3 11.7 %cholesky.50 = f32[128,128]{1,0:T(8,128)S(1)} custom-call(f32[128,128]{1,0:T(8,128)S(1)} %cholesky.118), custom_call_target="Cholesky" | custom-call | tf_op jit(solution)/shard_map/jit(cholesky)/cholesky | solution.py:49
  218.1 9.8 %custom-call.14 = f32[1,128,128]{1,2,0:T(8,128)S(1)} custom-call(f32[1,128,128]{2,1,0:T(8,128)S(1)} %get-tuple-element.28), custom_call_target="InvertDiagBlocksLowerTriangular" | custom-call | tf_op jit(solution)/shard_map/jit(cholesky)/cholesky | solution.py:49
  228.4 11.9 %cholesky.105 = f32[128,128]{1,0:T(8,128)S(1)} custom-call(f32[128,128]{1,0:T(8,128)S(1)} %convolution_subtract_fusion.1), custom_call_target="Cholesky" | custom-call | tf_op jit(solution)/shard_map/jit(cholesky)/cholesky | solution.py:49
  242.3 3.8 %while.1 = (s32[]{:T(128)}, f32[256,256]{1,0:T(8,128)S(1)}, s32[2,2]{1,0:T(2,128)S(1)}, f32[2,128,128]{2,1,0:T(8,128)S(1)}, s32[]{:T(128)}) while((s32[]{:T(128)}, f32[256,256]{1,0:T(8,128)S(1)}, s32[2,2]{1,0:T(2,128)S(1)}, f32[2,128,128]{2,1,0:T(8,128)S(1)}, s32[]{:T(128)}) %tuple.28), condition=%wide.while_cond, body=%wide.while_body.sunk | while | flops 2 | bytes 131181 | solution.py:50
  246.1 19.7 %custom-call.15 = f32[2,128,128]{1,2,0:T(8,128)S(1)} custom-call(f32[2,128,128]{2,1,0:T(8,128)S(1)} %get-tuple-element.14), custom_call_target="InvertDiagBlocksLowerTriangular" | custom-call | tf_op jit(solution)/shard_map/triangular_solve | solution.py:50
  268.5 1.5 pad_maximum_fusion
  (109 shorter events, 31.4 us)
Async XLA Ops:
  6.5 195.7 %all-gather.3.cloned.1.call-start = ((), (), s32[]{:S(2)}) async-start(), calls=%async_computation | async-start | bytes 8650752 | tf_op jit(solution)/shard_map/all_gather | solution.py:49
  9.5 9.4 %collective-permute-start = (bf16[1,1,64,2,256]{4,2,3,1,0:T(8,128)(2,1)S(1)}, bf16[1,1,64,2,256]{4,2,3,1,0:T(8,128)(2,1)S(1)}, u32[]{:S(2)}, u32[]{:S(2)}) collective-permute-start(bf16[1,1,64,2,256]{4,2,3,1,0:T(8,128)(2,1)S(1)} %select_bitcast_fusion.3), channel_id=1, source_target_pairs={{0,8},{8,16},{16,24},{1,9},{9,17},{17,25},{2,10},{10,18},{18,26},{... | collective-permute-start | bytes 196616 | tf_op jit(solution)/shard_map/ppermute | solution.py:12
  14.3 6.2 %collective-permute-start.1 = (bf16[1,1,64,2,256]{4,2,3,1,0:T(8,128)(2,1)S(1)}, bf16[1,1,64,2,256]{4,2,3,1,0:T(8,128)(2,1)S(1)}, u32[]{:S(2)}, u32[]{:S(2)}) collective-permute-start(bf16[1,1,64,2,256]{4,2,3,1,0:T(8,128)(2,1)S(1)} %select_bitcast_fusion.3), channel_id=1, source_target_pairs={{8,0},{16,8},{24,16},{9,1},{17,9},{25,17},{10,2},{18,10},{26,18},{... | collective-permute-start | bytes 196616 | tf_op jit(solution)/shard_map/ppermute | solution.py:15
  20.5 2.6 collective-permute-start.2
  21.8 5.1 %collective-permute-start.3 = (bf16[3,1,64,2,256]{4,2,3,1,0:T(8,128)(2,1)S(1)}, bf16[3,1,64,2,256]{4,2,3,1,0:T(8,128)(2,1)S(1)}, u32[]{:S(2)}, u32[]{:S(2)}) collective-permute-start(bf16[3,1,64,2,256]{4,2,3,1,0:T(8,128)(2,1)S(1)} %pad_maximum_fusion.1), channel_id=1, source_target_pairs={{1,0},{2,1},{3,2},{4,3},{5,4},{6,5},{7,6},{9,8},{10,9},{11,10},{12... | collective-permute-start | bytes 589832 | tf_op jit(solution)/shard_map/ppermute | solution.py:15
  28.1 7.3 %copy-start.5 = (bf16[64,2048]{1,0:T(8,128)(2,1)S(1)}, bf16[64,2048]{1,0:T(8,128)(2,1)}, u32[]{:S(2)}) copy-start(bf16[64,2048]{1,0:T(8,128)(2,1)} %param.9) | copy-start | bytes 786436
  36.7 6.2 %collective-permute-start.4 = (bf16[1,1,64,2,256]{4,2,3,1,0:T(8,128)(2,1)S(1)}, bf16[1,1,64,2,256]{4,2,3,1,0:T(8,128)(2,1)S(1)}, u32[]{:S(2)}, u32[]{:S(2)}) collective-permute-start(bf16[1,1,64,2,256]{4,2,3,1,0:T(8,128)(2,1)S(1)} %select_bitcast_fusion.2), channel_id=1, source_target_pairs={{0,8},{8,16},{16,24},{1,9},{9,17},{17,25},{2,10},{10,18},{18,26},{... | collective-permute-start | bytes 196616 | tf_op jit(solution)/shard_map/ppermute | solution.py:12
  41.0 6.6 %collective-permute-start.5 = (bf16[1,1,64,2,256]{4,2,3,1,0:T(8,128)(2,1)S(1)}, bf16[1,1,64,2,256]{4,2,3,1,0:T(8,128)(2,1)S(1)}, u32[]{:S(2)}, u32[]{:S(2)}) collective-permute-start(bf16[1,1,64,2,256]{4,2,3,1,0:T(8,128)(2,1)S(1)} %select_bitcast_fusion.2), channel_id=1, source_target_pairs={{8,0},{16,8},{24,16},{9,1},{17,9},{25,17},{10,2},{18,10},{26,18},{... | collective-permute-start | bytes 196616 | tf_op jit(solution)/shard_map/ppermute | solution.py:15
  47.6 5.6 %collective-permute-start.6 = (bf16[3,1,64,2,256]{4,2,3,1,0:T(8,128)(2,1)S(1)}, bf16[3,1,64,2,256]{4,2,3,1,0:T(8,128)(2,1)S(1)}, u32[]{:S(2)}, u32[]{:S(2)}) collective-permute-start(bf16[3,1,64,2,256]{4,2,3,1,0:T(8,128)(2,1)S(1)} %pad_maximum_fusion.2), channel_id=1, source_target_pairs={{0,1},{1,2},{2,3},{3,4},{4,5},{5,6},{6,7},{8,9},{9,10},{10,11},{11... | collective-permute-start | bytes 589832 | tf_op jit(solution)/shard_map/ppermute | solution.py:12
  51.8 4.2 %collective-permute-start.7 = (bf16[3,1,64,2,256]{4,2,3,1,0:T(8,128)(2,1)S(1)}, bf16[3,1,64,2,256]{4,2,3,1,0:T(8,128)(2,1)S(1)}, u32[]{:S(2)}, u32[]{:S(2)}) collective-permute-start(bf16[3,1,64,2,256]{4,2,3,1,0:T(8,128)(2,1)S(1)} %pad_maximum_fusion.2), channel_id=1, source_target_pairs={{1,0},{2,1},{3,2},{4,3},{5,4},{6,5},{7,6},{9,8},{10,9},{11,10},{12... | collective-permute-start | bytes 589832 | tf_op jit(solution)/shard_map/ppermute | solution.py:15
  65.1 19.6 %copy-start = (bf16[64,2048]{1,0:T(8,128)(2,1)}, bf16[64,2048]{1,0:T(8,128)(2,1)S(1)}, u32[]{:S(2)}) copy-start(bf16[64,2048]{1,0:T(8,128)(2,1)S(1)} %subtract_convert_fusion.2) | copy-start | bytes 786436
  65.8 5.7 %collective-permute-start.8 = (bf16[1,1,64,2,256]{4,2,3,1,0:T(8,128)(2,1)S(1)}, bf16[1,1,64,2,256]{4,2,3,1,0:T(8,128)(2,1)S(1)}, u32[]{:S(2)}, u32[]{:S(2)}) collective-permute-start(bf16[1,1,64,2,256]{4,2,3,1,0:T(8,128)(2,1)S(1)} %select_bitcast_fusion.1), channel_id=1, source_target_pairs={{0,8},{8,16},{16,24},{1,9},{9,17},{17,25},{2,10},{10,18},{18,26},{... | collective-permute-start | bytes 196616 | tf_op jit(solution)/shard_map/ppermute | solution.py:12
  69.6 6.4 %collective-permute-start.9 = (bf16[1,1,64,2,256]{4,2,3,1,0:T(8,128)(2,1)S(1)}, bf16[1,1,64,2,256]{4,2,3,1,0:T(8,128)(2,1)S(1)}, u32[]{:S(2)}, u32[]{:S(2)}) collective-permute-start(bf16[1,1,64,2,256]{4,2,3,1,0:T(8,128)(2,1)S(1)} %select_bitcast_fusion.1), channel_id=1, source_target_pairs={{8,0},{16,8},{24,16},{9,1},{17,9},{25,17},{10,2},{18,10},{26,18},{... | collective-permute-start | bytes 196616 | tf_op jit(solution)/shard_map/ppermute | solution.py:15
  76.1 5.7 %collective-permute-start.10 = (bf16[3,1,64,2,256]{4,2,3,1,0:T(8,128)(2,1)S(1)}, bf16[3,1,64,2,256]{4,2,3,1,0:T(8,128)(2,1)S(1)}, u32[]{:S(2)}, u32[]{:S(2)}) collective-permute-start(bf16[3,1,64,2,256]{4,2,3,1,0:T(8,128)(2,1)S(1)} %pad_maximum_fusion.3), channel_id=1, source_target_pairs={{0,1},{1,2},{2,3},{3,4},{4,5},{5,6},{6,7},{8,9},{9,10},{10,11},{11... | collective-permute-start | bytes 589832 | tf_op jit(solution)/shard_map/ppermute | solution.py:12
  80.5 4.2 %collective-permute-start.11 = (bf16[3,1,64,2,256]{4,2,3,1,0:T(8,128)(2,1)S(1)}, bf16[3,1,64,2,256]{4,2,3,1,0:T(8,128)(2,1)S(1)}, u32[]{:S(2)}, u32[]{:S(2)}) collective-permute-start(bf16[3,1,64,2,256]{4,2,3,1,0:T(8,128)(2,1)S(1)} %pad_maximum_fusion.3), channel_id=1, source_target_pairs={{1,0},{2,1},{3,2},{4,3},{5,4},{6,5},{7,6},{9,8},{10,9},{11,10},{12... | collective-permute-start | bytes 589832 | tf_op jit(solution)/shard_map/ppermute | solution.py:15
  85.8 7.3 %copy-start.1 = (bf16[64,2048]{1,0:T(8,128)(2,1)S(1)}, bf16[64,2048]{1,0:T(8,128)(2,1)}, u32[]{:S(2)}) copy-start(bf16[64,2048]{1,0:T(8,128)(2,1)} %copy-done) | copy-start | bytes 786436
  93.9 18.4 %copy-start.3 = (bf16[64,2048]{1,0:T(8,128)(2,1)}, bf16[64,2048]{1,0:T(8,128)(2,1)S(1)}, u32[]{:S(2)}) copy-start(bf16[64,2048]{1,0:T(8,128)(2,1)S(1)} %subtract_convert_fusion.1) | copy-start | bytes 786436
  94.6 4.6 %collective-permute-start.12 = (bf16[1,1,64,2,256]{4,2,3,1,0:T(8,128)(2,1)S(1)}, bf16[1,1,64,2,256]{4,2,3,1,0:T(8,128)(2,1)S(1)}, u32[]{:S(2)}, u32[]{:S(2)}) collective-permute-start(bf16[1,1,64,2,256]{4,2,3,1,0:T(8,128)(2,1)S(1)} %select_bitcast_fusion), channel_id=1, source_target_pairs={{0,8},{8,16},{16,24},{1,9},{9,17},{17,25},{2,10},{10,18},{18,26},{... | collective-permute-start | bytes 196616 | tf_op jit(solution)/shard_map/ppermute | solution.py:12
  97.3 6.4 %collective-permute-start.13 = (bf16[1,1,64,2,256]{4,2,3,1,0:T(8,128)(2,1)S(1)}, bf16[1,1,64,2,256]{4,2,3,1,0:T(8,128)(2,1)S(1)}, u32[]{:S(2)}, u32[]{:S(2)}) collective-permute-start(bf16[1,1,64,2,256]{4,2,3,1,0:T(8,128)(2,1)S(1)} %select_bitcast_fusion), channel_id=1, source_target_pairs={{8,0},{16,8},{24,16},{9,1},{17,9},{25,17},{10,2},{18,10},{26,18},{... | collective-permute-start | bytes 196616 | tf_op jit(solution)/shard_map/ppermute | solution.py:15
  103.7 5.9 %collective-permute-start.14 = (bf16[3,1,64,2,256]{4,2,3,1,0:T(8,128)(2,1)S(1)}, bf16[3,1,64,2,256]{4,2,3,1,0:T(8,128)(2,1)S(1)}, u32[]{:S(2)}, u32[]{:S(2)}) collective-permute-start(bf16[3,1,64,2,256]{4,2,3,1,0:T(8,128)(2,1)S(1)} %pad_maximum_fusion.4), channel_id=1, source_target_pairs={{0,1},{1,2},{2,3},{3,4},{4,5},{5,6},{6,7},{8,9},{9,10},{10,11},{11... | collective-permute-start | bytes 589832 | tf_op jit(solution)/shard_map/ppermute | solution.py:12
  108.1 4.2 %collective-permute-start.15 = (bf16[3,1,64,2,256]{4,2,3,1,0:T(8,128)(2,1)S(1)}, bf16[3,1,64,2,256]{4,2,3,1,0:T(8,128)(2,1)S(1)}, u32[]{:S(2)}, u32[]{:S(2)}) collective-permute-start(bf16[3,1,64,2,256]{4,2,3,1,0:T(8,128)(2,1)S(1)} %pad_maximum_fusion.4), channel_id=1, source_target_pairs={{1,0},{2,1},{3,2},{4,3},{5,4},{6,5},{7,6},{9,8},{10,9},{11,10},{12... | collective-permute-start | bytes 589832 | tf_op jit(solution)/shard_map/ppermute | solution.py:15
  113.4 7.4 %copy-start.4 = (bf16[64,2048]{1,0:T(8,128)(2,1)S(1)}, bf16[64,2048]{1,0:T(8,128)(2,1)}, u32[]{:S(2)}) copy-start(bf16[64,2048]{1,0:T(8,128)(2,1)} %copy-done.3) | copy-start | bytes 786436
  113.4 8.1 %copy-start.2 = (bf16[64,2048]{1,0:T(8,128)(2,1)S(1)}, bf16[64,2048]{1,0:T(8,128)(2,1)}, u32[]{:S(2)}) copy-start(bf16[64,2048]{1,0:T(8,128)(2,1)} %copy-done) | copy-start | bytes 786436
Sparse Core Ops, SparseCore 0:
  122.8 79.3 all-gather.2
